TPU v7x, 32 devices: a whole 2x2x4 slice. The times are simulated.
32 devices in a mesh: dp: 2 (over x), row: 4 (over z), col: 4 (over y, core).
Axes of the slice: x: 2, y: 2, z: 4, core: 2. Of those that a mesh axis runs over, the one named last changes fastest.
Arguments:
- tokens: bfloat16 [16, 768, 1024], P(('dp', 'row'), 'col'), may hold values from -6 to 6
- memory: bfloat16 [16, 20, 768], P(('dp', 'row'), None, 'col'), may hold values from -6 to 6
- block_ids: int32 [16, 1024], P(('dp', 'row')), may hold values from 0 to 7, never falling along the last dimension, each value on 1 to 256 neighbouring positions
- valid: int32 [16], replicated, may hold values from 512 to 1024
- teacher: bfloat16 [16, 768, 1024], P(('dp', 'row'), 'col'), may hold values from -6 to 6
- w_qkv: bfloat16 [12, 147456], P('row', 'col'), may hold values from -0.21875 to 0.21875
- bias_qv: float32 [12, 128], P('row'), may hold values from -3 to 3
- w_out: bfloat16 [768, 768], P('row', 'col'), may hold values from -0.875 to 0.875
- bias_out: float32 [768], P('col'), may hold values from -2 to 2
- ln1_gain: float32 [768], P('col'), may hold values from 0.1 to 1.9
- ln1_bias: float32 [768], P('col'), may hold values from -2 to 2
- w_up: bfloat16 [768, 3072], P('col', 'row'), may hold values from -0.21875 to 0.21875
- bias_up: float32 [3072], P('row'), may hold values from -3 to 3
- w_down: bfloat16 [768, 3072], P('col', 'row'), may hold values from -0.109375 to 0.109375
- bias_down: float32 [768], P('col'), may hold values from -2 to 2
- ln2_gain: float32 [768], P('col'), may hold values from 0.1 to 1.9
- ln2_bias: float32 [768], P('col'), may hold values from -2 to 2
Outputs:
- layer_out: bfloat16 [16, 1044, 768], P(('dp', 'row'), None, 'col')
- grad_tokens: float32 [16, 1024, 768], P(('dp', 'row'), None, 'col')
- grad_memory: float32 [16, 20, 768], P(('dp', 'row'), None, 'col')
- grad_w_qkv: float32 [12, 147456], P('row', 'col')
- grad_bias_qv: float32 [12, 128], P('row')
- grad_w_out: float32 [768, 768], P('row', 'col')
- grad_bias_out: float32 [768], P('col')
- grad_ln1_gain: float32 [768], P('col')
- grad_ln1_bias: float32 [768], P('col')
- grad_w_up: float32 [768, 3072], P('col', 'row')
- grad_bias_up: float32 [3072], P('row')
- grad_w_down: float32 [768, 3072], P('col', 'row')
- grad_bias_down: float32 [768], P('col')
- grad_ln2_gain: float32 [768], P('col')
- grad_ln2_bias: float32 [768], P('col')
Inputs may be any that keep to these rules, and one draw needn't show every extreme that they name: `block_ids`: along each sequence the numbers never fall; each of the 8 numbers covers 1 to 256 consecutive tokens.
All inputs are finite; a program needn't handle non-finite values.
Results may differ from a plain program's by a relative error of at most 0.015.
Values may be sent and summed in bfloat16 or wider, within the bound.
A program may use at most 192 MiB of HBM per device.

v0:
```python
from functools import partial
import jax
import jax.numpy as jnp
from jax import lax
from jax.sharding import PartitionSpec as P

EPSILON = 1e-12
NEGATIVE = -1e30


def gather_feats(shard):
    return lax.all_gather(shard, "col", axis=1, tiled=True)


def back_gather(shard):
    return lax.all_gather(shard, "col", axis=1, tiled=True)


def forward_reduce(partial_rows):
    return lax.psum_scatter(
        partial_rows.astype(jnp.bfloat16), "col", scatter_dimension=1, tiled=True
    ).astype(jnp.float32)


def backward_reduce(partial_rows):
    return lax.psum_scatter(
        partial_rows.astype(jnp.bfloat16), "col", scatter_dimension=1, tiled=True
    ).astype(jnp.float32)


def against(piece_rows, matrix):
    return lax.dot_general(
        piece_rows, matrix, (((1,), (1,)), ((), ())), preferred_element_type=jnp.float32
    )


def column_total(piece_rows):
    unit_row = jnp.ones((1, piece_rows.shape[0]), jnp.bfloat16)
    return jnp.dot(unit_row, piece_rows, preferred_element_type=jnp.float32)[0]


def outer_sum(left_rows, right_rows):
    return lax.dot_general(
        left_rows, right_rows, (((0,), (0,)), ((), ())), preferred_element_type=jnp.float32
    )


def assemble(stacked, row_size, col_size):
    shape = stacked.shape
    grid = stacked.reshape((row_size, col_size) + shape[1:])
    moved = jnp.swapaxes(grid, 1, 2)
    return moved.reshape((row_size * shape[1], col_size * shape[2]) + shape[3:])


def norm_forward(summed, gain, shift, feat_total):
    sum_plain, sum_square = lax.psum(
        (jnp.sum(summed, axis=1), jnp.sum(summed * summed, axis=1)), "col"
    )
    average = sum_plain / feat_total
    inverse = lax.rsqrt(sum_square / feat_total - average * average + EPSILON)
    scaled = (summed - average[:, None]) * inverse[:, None]
    return (scaled * gain + shift, scaled, inverse)


def norm_backward(cotangent, scaled, inverse, gain, feat_total):
    weighted = cotangent * gain
    sum_plain, sum_cross = lax.psum(
        (jnp.sum(weighted, axis=1), jnp.sum(weighted * scaled, axis=1)), "col"
    )
    inner = weighted - sum_plain[:, None] / feat_total - scaled * (sum_cross[:, None] / feat_total)
    return (
        inverse[:, None] * inner,
        jnp.sum(cotangent * scaled, axis=0),
        jnp.sum(cotangent, axis=0),
    )


def visible_rows(token_ids, seq_rows):
    length = token_ids.shape[0]
    memory_rows = (seq_rows - length) // 2
    row_ids = jnp.concatenate(
        [
            jnp.full((memory_rows,), -1, jnp.int32),
            token_ids,
            jnp.full((memory_rows,), length, jnp.int32),
        ]
    )
    return row_ids[None, :] <= row_ids[:, None]


def masked_scores(queries, key_rows, token_ids):
    inv_root = queries.shape[-1] ** (-0.5)
    scores = (
        jnp.einsum("qhe,khe->hqk", queries, key_rows, preferred_element_type=jnp.float32) * inv_root
    )
    visible = visible_rows(token_ids, queries.shape[0])
    return jnp.where(visible[None], scores, NEGATIVE)


def attend(packed):
    queries, key_rows, values, token_ids = packed
    masked = masked_scores(queries, key_rows, token_ids)
    highest = jnp.max(masked, axis=-1, keepdims=True)
    exponent = jnp.exp(masked - highest)
    summed = jnp.sum(exponent, axis=-1, keepdims=True)
    attn_weights = (exponent / summed).astype(jnp.bfloat16)
    mixed_out = jnp.einsum("hqk,khe->qhe", attn_weights, values, preferred_element_type=jnp.float32)
    return (mixed_out.astype(jnp.bfloat16), (highest + jnp.log(summed))[..., 0])


def attend_back(packed):
    queries, key_rows, values, token_ids, log_totals, grad_mixed = packed
    inv_root = queries.shape[-1] ** (-0.5)
    masked = masked_scores(queries, key_rows, token_ids)
    probs_full = jnp.exp(masked - log_totals[..., None])
    attn_weights = probs_full.astype(jnp.bfloat16)
    grad_probs = jnp.einsum("qhe,khe->hqk", grad_mixed, values, preferred_element_type=jnp.float32)
    row_inner = jnp.sum(probs_full * grad_probs, axis=-1, keepdims=True)
    grad_scores = (probs_full * (grad_probs - row_inner)).astype(jnp.bfloat16)
    grad_queries = (
        jnp.einsum("hqk,khe->qhe", grad_scores, key_rows, preferred_element_type=jnp.float32)
        * inv_root
    )
    grad_keys = (
        jnp.einsum("hqk,qhe->khe", grad_scores, queries, preferred_element_type=jnp.float32)
        * inv_root
    )
    grad_values = jnp.einsum(
        "hqk,qhe->khe", attn_weights, grad_mixed, preferred_element_type=jnp.float32
    )
    return (
        grad_queries.astype(jnp.bfloat16),
        grad_keys.astype(jnp.bfloat16),
        grad_values.astype(jnp.bfloat16),
    )


def per_device(
    tokens,
    memory,
    block_ids,
    valid,
    teacher,
    w_qkv,
    bias_qv,
    w_out,
    bias_out,
    ln1_gain,
    ln1_bias,
    w_up,
    bias_up,
    w_down,
    bias_down,
    ln2_gain,
    ln2_bias,
):
    seq_count, feat_cols, length = tokens.shape
    memory_rows = memory.shape[1] // 2
    seq_rows = length + 2 * memory_rows
    row_count = seq_count * seq_rows
    row_size = lax.axis_size("row")
    col_size = lax.axis_size("col")
    row_place = lax.axis_index("row")
    col_place = lax.axis_index("col")
    head_rows = w_qkv.shape[0]
    head_size = bias_qv.shape[1] // 2
    feat_total = feat_cols * col_size
    head_local = head_rows * row_size // col_size
    unit_total = bias_up.shape[0] * row_size
    unit_local = unit_total // col_size
    qkv_blocks = w_qkv.reshape(head_rows, feat_cols, 3 * head_size)
    up_blocks = jnp.transpose(w_up)
    down_blocks = jnp.transpose(w_down)
    whole = (
        lax.all_gather(qkv_blocks[None], ("row", "col"), axis=0, tiled=True),
        lax.all_gather(w_out[None], ("row", "col"), axis=0, tiled=True),
        lax.all_gather(up_blocks[None], ("row", "col"), axis=0, tiled=True),
        lax.all_gather(down_blocks[None], ("row", "col"), axis=0, tiled=True),
    )
    full_qkv = assemble(whole[0], row_size, col_size)
    full_out = assemble(whole[1], row_size, col_size)
    full_up = assemble(whole[2], row_size, col_size)
    full_down = assemble(whole[3], row_size, col_size)
    qkv_heads = lax.dynamic_slice_in_dim(full_qkv, col_place * head_local, head_local, 0)
    out_rows = lax.dynamic_slice_in_dim(
        full_out, col_place * (head_local * head_size), head_local * head_size, 0
    )
    up_rows = lax.dynamic_slice_in_dim(full_up, col_place * unit_local, unit_local, 0)
    down_rows = lax.dynamic_slice_in_dim(full_down, col_place * unit_local, unit_local, 0)
    bias_heads_all, bias_units_all = (
        lax.all_gather(bias_qv, "row", axis=0, tiled=True),
        lax.all_gather(bias_up, "row", axis=0, tiled=True),
    )
    bias_heads = lax.dynamic_slice_in_dim(bias_heads_all, col_place * head_local, head_local, 0)
    bias_units = lax.dynamic_slice_in_dim(bias_units_all, col_place * unit_local, unit_local, 0)
    flat_qkv = jnp.transpose(qkv_heads, (1, 0, 2)).reshape(feat_total, head_local * 3 * head_size)
    token_rows = jnp.swapaxes(tokens, 1, 2)
    inputs = jnp.concatenate(
        [memory[:, :memory_rows], token_rows, memory[:, memory_rows:]], axis=1
    ).reshape(row_count, feat_cols)
    full_in = gather_feats(inputs)
    projected = jnp.dot(full_in, flat_qkv, preferred_element_type=jnp.float32).reshape(
        seq_count, seq_rows, head_local, 3 * head_size
    )
    queries = (projected[..., :head_size] + bias_heads[:, :head_size]).astype(jnp.bfloat16)
    key_rows = projected[..., head_size : 2 * head_size].astype(jnp.bfloat16)
    values = (projected[..., 2 * head_size :] + bias_heads[:, head_size:]).astype(jnp.bfloat16)
    mixed_out, log_totals = lax.map(attend, (queries, key_rows, values, block_ids))
    mixed_rows = mixed_out.reshape(row_count, head_local * head_size)
    attn_out = (
        forward_reduce(jnp.dot(mixed_rows, out_rows, preferred_element_type=jnp.float32)) + bias_out
    )
    norm_one, scaled_one, inverse_one = norm_forward(
        inputs.astype(jnp.float32) + attn_out, ln1_gain, ln1_bias, feat_total
    )
    norm_low = norm_one.astype(jnp.bfloat16)
    full_norm = gather_feats(norm_low)
    gate_pre = against(full_norm, up_rows) + bias_units
    hidden = jax.nn.gelu(gate_pre, approximate=False).astype(jnp.bfloat16)
    branch = (
        forward_reduce(jnp.dot(hidden, down_rows, preferred_element_type=jnp.float32)) + bias_down
    )
    output_rows, scaled_two, inverse_two = norm_forward(
        norm_one + branch, ln2_gain, ln2_bias, feat_total
    )
    output_seq = output_rows.reshape(seq_count, seq_rows, feat_cols)
    offset = lax.axis_index(("dp", "row")) * seq_count
    counts = lax.dynamic_slice_in_dim(valid, offset, seq_count, 0)
    loss_scale = valid.shape[0] * length / jnp.sum(valid).astype(jnp.float32)
    kept_rows = (jnp.arange(length, dtype=jnp.int32)[None, :] < counts[:, None])[..., None]
    mismatch = output_seq[:, memory_rows : memory_rows + length] - jnp.swapaxes(
        teacher, 1, 2
    ).astype(jnp.float32)
    grad_tok = jnp.where(kept_rows, loss_scale * mismatch, 0.0)
    grad_out = jnp.pad(grad_tok, ((0, 0), (memory_rows, memory_rows), (0, 0))).reshape(
        row_count, feat_cols
    )
    grad_two, gain_two, shift_two = norm_backward(
        grad_out, scaled_two, inverse_two, ln2_gain, feat_total
    )
    grad_branch = grad_two.astype(jnp.bfloat16)
    full_branch = back_gather(grad_branch)
    grad_down_rows = outer_sum(hidden, full_branch)
    grad_bias_down = column_total(grad_branch)
    grad_hidden = against(full_branch, down_rows)
    gelu_pull = jax.vjp(partial(jax.nn.gelu, approximate=False), gate_pre)[1]
    grad_gate = gelu_pull(grad_hidden)[0].astype(jnp.bfloat16)
    grad_up_rows = outer_sum(grad_gate, full_norm)
    grad_bias_units = column_total(grad_gate)
    grad_first = grad_two + backward_reduce(
        jnp.dot(grad_gate, up_rows, preferred_element_type=jnp.float32)
    )
    grad_one, gain_one, shift_one = norm_backward(
        grad_first, scaled_one, inverse_one, ln1_gain, feat_total
    )
    grad_attn = grad_one.astype(jnp.bfloat16)
    full_attn = back_gather(grad_attn)
    grad_out_rows = outer_sum(mixed_rows, full_attn)
    grad_bias_out = column_total(grad_attn)
    grad_mixed = against(full_attn, out_rows).astype(jnp.bfloat16)
    grad_mixed = grad_mixed.reshape(seq_count, seq_rows, head_local, head_size)
    grad_queries, grad_keys, grad_values = lax.map(
        attend_back, (queries, key_rows, values, block_ids, log_totals, grad_mixed)
    )
    grad_proj = jnp.concatenate([grad_queries, grad_keys, grad_values], axis=-1).reshape(
        row_count, head_local * 3 * head_size
    )
    grad_flat = outer_sum(full_in, grad_proj).reshape(feat_total, head_local, 3 * head_size)
    grad_heads = jnp.transpose(grad_flat, (1, 0, 2))
    proj_total = column_total(grad_proj).reshape(head_local, 3 * head_size)
    grad_bias_heads = jnp.concatenate(
        [proj_total[:, :head_size], proj_total[:, 2 * head_size :]], axis=1
    )
    grad_in = grad_one + backward_reduce(against(grad_proj, flat_qkv))
    relayed = (
        lax.all_to_all(
            grad_heads.astype(jnp.bfloat16), "col", split_axis=1, concat_axis=0, tiled=True
        ).astype(grad_heads.dtype),
        lax.all_to_all(
            grad_out_rows.astype(jnp.bfloat16), "col", split_axis=1, concat_axis=0, tiled=True
        ).astype(grad_out_rows.dtype),
        lax.all_to_all(
            grad_up_rows.astype(jnp.bfloat16), "col", split_axis=1, concat_axis=0, tiled=True
        ).astype(grad_up_rows.dtype),
        lax.all_to_all(
            grad_down_rows.astype(jnp.bfloat16), "col", split_axis=1, concat_axis=0, tiled=True
        ).astype(grad_down_rows.dtype),
    )
    grid_parts = (
        lax.psum_scatter(
            relayed[0].astype(jnp.bfloat16), "row", scatter_dimension=0, tiled=True
        ).astype(jnp.float32),
        lax.psum_scatter(
            relayed[1].astype(jnp.bfloat16), "row", scatter_dimension=0, tiled=True
        ).astype(jnp.float32),
        lax.psum_scatter(
            relayed[2].astype(jnp.bfloat16), "row", scatter_dimension=0, tiled=True
        ).astype(jnp.float32),
        lax.psum_scatter(
            relayed[3].astype(jnp.bfloat16), "row", scatter_dimension=0, tiled=True
        ).astype(jnp.float32),
    )
    weight_totals = (
        lax.psum(grid_parts[0].astype(jnp.bfloat16), "dp").astype(jnp.float32),
        lax.psum(grid_parts[1].astype(jnp.bfloat16), "dp").astype(jnp.float32),
        lax.psum(grid_parts[2].astype(jnp.bfloat16), "dp").astype(jnp.float32),
        lax.psum(grid_parts[3].astype(jnp.bfloat16), "dp").astype(jnp.float32),
    )
    grad_w_qkv = weight_totals[0].reshape(head_rows, feat_cols * 3 * head_size)
    grad_w_out = weight_totals[1]
    grad_w_up = jnp.transpose(weight_totals[2])
    grad_w_down = jnp.transpose(weight_totals[3])
    heads_pad = lax.dynamic_update_slice_in_dim(
        jnp.zeros((head_local * col_size, 2 * head_size), jnp.float32),
        grad_bias_heads,
        col_place * head_local,
        0,
    )
    units_pad = lax.dynamic_update_slice_in_dim(
        jnp.zeros((unit_total,), jnp.float32), grad_bias_units, col_place * unit_local, 0
    )
    feat_stack = jnp.stack(
        [gain_one, shift_one, gain_two, shift_two, grad_bias_out, grad_bias_down]
    )
    feat_pad = lax.dynamic_update_slice_in_dim(
        jnp.zeros((6, feat_total), jnp.float32), feat_stack, col_place * feat_cols, 1
    )
    small_totals = lax.psum((heads_pad, units_pad, feat_pad), ("dp", "row", "col"))
    grad_bias_qv = lax.dynamic_slice_in_dim(small_totals[0], row_place * head_rows, head_rows, 0)
    grad_bias_up = lax.dynamic_slice_in_dim(
        small_totals[1], row_place * bias_up.shape[0], bias_up.shape[0], 0
    )
    feat_totals = lax.dynamic_slice_in_dim(small_totals[2], col_place * feat_cols, feat_cols, 1)
    grad_seq = grad_in.reshape(seq_count, seq_rows, feat_cols)
    grad_tokens = grad_seq[:, memory_rows : memory_rows + length]
    grad_memory = jnp.concatenate(
        [grad_seq[:, :memory_rows], grad_seq[:, memory_rows + length :]], axis=1
    )
    return (
        output_seq.astype(jnp.bfloat16),
        grad_tokens,
        grad_memory,
        grad_w_qkv,
        grad_bias_qv,
        grad_w_out,
        feat_totals[4],
        feat_totals[0],
        feat_totals[1],
        grad_w_up,
        grad_bias_up,
        grad_w_down,
        feat_totals[5],
        feat_totals[2],
        feat_totals[3],
    )


def solution(mesh):
    in_specs = (
        P(("dp", "row"), "col", None),
        P(("dp", "row"), None, "col"),
        P(("dp", "row"), None),
        P(),
        P(("dp", "row"), "col", None),
        P("row", "col"),
        P("row", None),
        P("row", "col"),
        P("col"),
        P("col"),
        P("col"),
        P("col", "row"),
        P("row"),
        P("col", "row"),
        P("col"),
        P("col"),
        P("col"),
    )
    out_specs = (
        P(("dp", "row"), None, "col"),
        P(("dp", "row"), None, "col"),
        P(("dp", "row"), None, "col"),
        P("row", "col"),
        P("row", None),
        P("row", "col"),
        P("col"),
        P("col"),
        P("col"),
        P("col", "row"),
        P("row"),
        P("col", "row"),
        P("col"),
        P("col"),
        P("col"),
    )
    return jax.shard_map(
        per_device, mesh=mesh, in_specs=in_specs, out_specs=out_specs, check_vma=False
    )
```

profile of v0, /device:TPU:0, one launch (start us, length us, event | category | flops | bytes accessed | tf_op | source)
XLA Modules:
  0.0 976.6 jit_solution(16924794278916850676)
XLA Ops:
  14.5 13.6 %all-gather.3 = f32[4,3,128]{2,1,0:T(4,128)S(1)} all-gather(f32[1,3,128]{2,1,0:T(4,128)S(1)} %bitcast.266), channel_id=1, replica_groups=mesh['dp'=2,'row'=4,'col'=4] {'row'}, dimensions={0}, use_global_device_ids=true | all-gather | bytes 7680 | tf_op jit(solution)/shard_map/all_gather | solution.py:191
  28.2 24.4 %all-gather.24.cloned.1.call-done = bf16[3072,192]{1,0:T(8,128)(2,1)} async-done(((bf16[192,192]{1,0:T(8,128)(2,1)}), bf16[3072,192]{1,0:T(8,128)(2,1)}) %all-gather.24.cloned.1.call-update) | async-done | bytes 1179664 | tf_op jit(solution)/shard_map/all_gather | solution.py:176
  57.5 25.1 %all-gather.14.cloned.1.call-done = bf16[2088,768]{0,1:T(8,128)(2,1)} async-done(((bf16[2088,192]{0,1:T(8,128)(2,1)}), bf16[2088,768]{0,1:T(8,128)(2,1)}) %all-gather.14.cloned.1.call-update) | async-done | bytes 3207184 | tf_op jit(solution)/shard_map/all_gather | solution.py:12
  82.5 8.7 reshape.275
  91.2 47.3 %all-gather.16.cloned.1.call-done = bf16[16,3,192,192]{3,2,1,0:T(8,128)(2,1)} async-done(((bf16[1,3,192,192]{3,2,1,0:T(8,128)(2,1)}), bf16[16,3,192,192]{3,2,1,0:T(8,128)(2,1)}) %all-gather.16.cloned.1.call-update) | async-done | bytes 3538960 | tf_op jit(solution)/shard_map/all_gather | solution.py:175
  138.5 9.7 copy.108
  148.2 7.7 reshape.238
  155.9 4.6 fusion.60
  161.4 51.5 %while.26 = (s32[]{:T(128)}, bf16[2,1044,3,64]{1,3,2,0:T(8,128)(2,1)S(1)}, f32[2,3,1044]{2,1,0:T(4,128)}, bf16[2,1044,3,64]{1,3,2,0:T(8,128)(2,1)S(1)}, s32[2,10...) while((s32[]{:T(128)}, ...), condition=%wide.region_3.4_spmd, body=%wide.region_0.3_spmd.sunk | while | flops 864516608 | bytes 43690424 | solution.py:208
  163.9 8.0 fusion.151
  171.9 7.1 fusion.152
  179.0 7.8 fusion.153
  189.4 8.0 fusion.151
  197.4 7.1 fusion.152
  204.5 7.8 fusion.153
  218.0 4.0 convolution_convert_fusion.3
  223.5 36.4 %reduce-scatter.9.cloned.1.call-done = bf16[2088,192]{0,1:T(8,128)(2,1)} async-done(((bf16[2088,768]{0,1:T(8,128)(2,1)}), bf16[2088,192]{0,1:T(8,128)(2,1)}) %reduce-scatter.9.cloned.1.call-update) | async-done | bytes 801808 | tf_op jit(solution)/shard_map/reduce_scatter | solution.py:20
  261.6 10.3 %all-reduce.5 = (f32[2088]{0:T(1024)S(1)}, f32[2088]{0:T(1024)S(1)}) all-reduce(f32[2088]{0:T(1024)S(1)} %get-tuple-element.158, f32[2088]{0:T(1024)S(1)} %get-tuple-element.157), channel_id=1, replica_groups=mesh['dp'=2,'row'=4,'col'=4] {'col'}, use_global_device_ids=true, to_apply=%region_8.9 | all-reduce | flops 4176 | bytes 33408 | tf_op jit(solution)/shard_map/psum | solution.py:56
  274.6 13.3 %all-gather.4 = f32[4,1,768]{2,1,0:T(1,128)S(1)} all-gather(f32[1,1,768]{2,1,0:T(1,128)S(1)} %reshape.262), channel_id=1, replica_groups=mesh['dp'=2,'row'=4,'col'=4] {'row'}, dimensions={0}, use_global_device_ids=true | all-gather | bytes 15360 | tf_op jit(solution)/shard_map/all_gather | solution.py:192
  288.0 27.5 %all-gather.26.cloned.1.call-done = bf16[12288,192]{0,1:T(8,128)(2,1)} async-done(((bf16[768,192]{0,1:T(8,128)(2,1)}), bf16[12288,192]{0,1:T(8,128)(2,1)}) %all-gather.26.cloned.1.call-update) | async-done | bytes 4718608 | tf_op jit(solution)/shard_map/all_gather | solution.py:177
  315.5 8.2 reshape.243
  323.7 4.3 copy.111
  328.0 3.2 copy.143
  331.2 38.2 %all-gather.28.cloned.1.call-done = bf16[12288,192]{0,1:T(8,128)(2,1)} async-done(((bf16[768,192]{0,1:T(8,128)(2,1)}), bf16[12288,192]{0,1:T(8,128)(2,1)}) %all-gather.28.cloned.1.call-update) | async-done | bytes 4718608 | tf_op jit(solution)/shard_map/all_gather | solution.py:178
  369.4 8.3 reshape.245
  377.7 4.7 copy.112
  385.5 14.0 %all-gather.18.cloned.1.call-done = bf16[2088,768]{0,1:T(8,128)(2,1)} async-done(((bf16[2088,192]{0,1:T(8,128)(2,1)}), bf16[2088,768]{0,1:T(8,128)(2,1)}) %all-gather.18.cloned.1.call-update) | async-done | bytes 3207184 | tf_op jit(solution)/shard_map/all_gather | solution.py:12
  399.5 20.0 %multiply_convert_fusion.1 = (bf16[2088,768]{1,0:T(8,128)(2,1)S(1)}, f32[2088,768]{1,0:T(8,128)}, f32[2088,768]{1,0:T(8,128)}) fusion(f32[768]{0:T(1024)S(1)} %dynamic_slice.67, bf16[2088,768]{0,1:T(8,128)(2,1)} %all-gather.18.cloned.1.call-done, bf16[3072,768]{0,1:T(8,128)(2,1)} %bitcast.237, s32[]{:T(128)S(6)} %select_n.38), kind=kOutput, calls=%fused_computation.65 | convolution fusion | flops 2568941568 | bytes 20560900 | tf_op jit(solution)/shard_map/dot_general | solution.py:32
  421.2 5.9 convolution_convert_fusion.2
  429.2 37.2 %reduce-scatter.11.cloned.1.call-done = bf16[2088,192]{0,1:T(8,128)(2,1)} async-done(((bf16[2088,768]{0,1:T(8,128)(2,1)}), bf16[2088,192]{0,1:T(8,128)(2,1)}) %reduce-scatter.11.cloned.1.call-update) | async-done | bytes 801808 | tf_op jit(solution)/shard_map/reduce_scatter | solution.py:20
  468.7 10.6 %all-reduce.4 = (f32[2088]{0:T(1024)S(1)}, f32[2088]{0:T(1024)S(1)}) all-reduce(f32[2088]{0:T(1024)S(1)} %get-tuple-element.161, f32[2088]{0:T(1024)S(1)} %get-tuple-element.160), channel_id=1, replica_groups=mesh['dp'=2,'row'=4,'col'=4] {'col'}, use_global_device_ids=true, to_apply=%region_13.14 | all-reduce | flops 4176 | bytes 33408 | tf_op jit(solution)/shard_map/psum | solution.py:56
  480.9 3.5 reshape.247
  490.3 4.5 pad.4.clone
  494.8 3.2 reshape.248
  500.5 10.3 %all-reduce.3 = (f32[2088]{0:T(1024)S(1)}, f32[2088]{0:T(1024)S(1)}) all-reduce(f32[2088]{0:T(1024)S(1)} %get-tuple-element.155, f32[2088]{0:T(1024)S(1)} %reduce_sum.143), channel_id=1, replica_groups=mesh['dp'=2,'row'=4,'col'=4] {'col'}, use_global_device_ids=true, to_apply=%region_18.19 | all-reduce | flops 4176 | bytes 33408 | tf_op jit(solution)/shard_map/psum | solution.py:67
  514.1 29.9 %all-gather.20.cloned.1.call-done = bf16[2088,768]{0,1:T(8,128)(2,1)} async-done(((bf16[2088,192]{0,1:T(8,128)(2,1)}), bf16[2088,768]{0,1:T(8,128)(2,1)}) %all-gather.20.cloned.1.call-update) | async-done | bytes 3207184 | tf_op jit(solution)/shard_map/all_gather | solution.py:16
  544.0 10.5 %add_convert_fusion = bf16[2088,768]{1,0:T(8,128)(2,1)S(1)} fusion(f32[2088,768]{1,0:T(8,128)} %get-tuple-element.216, f32[2088,768]{1,0:T(8,128)} %get-tuple-element.241, bf16[2088,768]{0,1:T(8,128)(2,1)} %all-gather.20.cloned.1.call-done, bf16[3072,768]{0,1:T(8,128)(2,1)} %bitcast.240, s32[]{:T(128)S(6)} %select_n.38), kind=kOutput, calls=%fused_computation.64 | convolution fusion | flops 2485555200 | bytes 20557828 | tf_op jit(solution)/shard_map/dot_general | solution.py:32
  556.2 6.0 convolution_convert_fusion.1
  562.3 39.2 %reduce-scatter.13.cloned.1.call-done = bf16[2088,192]{0,1:T(8,128)(2,1)} async-done(((bf16[2088,768]{0,1:T(8,128)(2,1)}), bf16[2088,192]{0,1:T(8,128)(2,1)}) %reduce-scatter.13.cloned.1.call-update) | async-done | bytes 801808 | tf_op jit(solution)/shard_map/reduce_scatter | solution.py:26
  601.5 5.0 multiply_reduce_fusion.3
  606.5 10.3 %all-reduce.2 = (f32[2088]{0:T(1024)S(1)}, f32[2088]{0:T(1024)S(1)}) all-reduce(f32[2088]{0:T(1024)S(1)} %get-tuple-element.153, f32[2088]{0:T(1024)S(1)} %get-tuple-element.156), channel_id=1, replica_groups=mesh['dp'=2,'row'=4,'col'=4] {'col'}, use_global_device_ids=true, to_apply=%region_23.24 | all-reduce | flops 4176 | bytes 33408 | tf_op jit(solution)/shard_map/psum | solution.py:67
  620.3 30.1 %all-gather.22.cloned.1.call-done = bf16[2088,768]{0,1:T(8,128)(2,1)} async-done(((bf16[2088,192]{0,1:T(8,128)(2,1)}), bf16[2088,768]{0,1:T(8,128)(2,1)}) %all-gather.22.cloned.1.call-update) | async-done | bytes 3207184 | tf_op jit(solution)/shard_map/all_gather | solution.py:16
  650.4 3.7 convolution_convert_fusion.4
  660.9 68.2 %while.27 = (s32[]{:T(128)}, bf16[2,1044,3,64]{1,3,2,0:T(8,128)(2,1)}, bf16[2,1044,3,64]{1,3,2,0:T(8,128)(2,1)}, bf16[2,1044,3,64]{1,3,2,0:T(8,128)(2,1)}, bf16[...) while((s32[]{:T(128)}, ...), condition=%wide.region_26.27_spmd, body=%wide.region_24.26_spmd.sunk | while | flops 2124194560 | bytes 151329200 | solution.py:262
  661.8 3.4 fusion.162
  665.2 8.2 multiply_reduce_fusion.10
  673.5 8.6 multiply_convert_fusion.3
  682.1 8.3 fusion.165
  695.8 3.4 fusion.162
  699.2 8.2 multiply_reduce_fusion.10
  707.5 8.6 multiply_convert_fusion.3
  716.0 8.3 fusion.165
  736.8 5.0 fusion.72
  742.7 22.5 %all_to_all.75 = bf16[3,768,192]{2,0,1:T(4,128)(2,1)S(1)} all-to-all(bf16[3,768,192]{2,0,1:T(4,128)(2,1)S(1)} %copy.121), channel_id=1, replica_groups=mesh['dp'=2,'row'=4,'col'=4] {'col'}, dimensions={1} | all-to-all | bytes 1769472 | tf_op jit(solution)/shard_map/all_to_all | solution.py:276
  767.6 4.8 convolution_convert_fusion.5
  772.4 18.5 %all_to_all.76 = bf16[768,4,192]{0,2,1:T(8,128)(2,1)S(1)} all-to-all(bf16[768,4,192]{0,2,1:T(8,128)(2,1)S(1)} %bitcast.250), channel_id=1, replica_groups=mesh['dp'=2,'row'=4,'col'=4] {'col'}, dimensions={1} | all-to-all | bytes 2359296 | tf_op jit(solution)/shard_map/all_to_all | solution.py:285
  792.2 4.9 convolution_convert_fusion.6
  797.1 18.4 %all_to_all.77 = bf16[768,4,192]{0,2,1:T(8,128)(2,1)S(1)} all-to-all(bf16[768,4,192]{0,2,1:T(8,128)(2,1)S(1)} %bitcast.251), channel_id=1, replica_groups=mesh['dp'=2,'row'=4,'col'=4] {'col'}, dimensions={1} | all-to-all | bytes 2359296 | tf_op jit(solution)/shard_map/all_to_all | solution.py:282
  820.7 10.6 %all_to_all.78 = bf16[192,4,192]{2,0,1:T(8,128)(2,1)} all-to-all(bf16[192,4,192]{2,0,1:T(8,128)(2,1)S(1)} %copy.124), channel_id=1, replica_groups=mesh['dp'=2,'row'=4,'col'=4] {'col'}, dimensions={1} | all-to-all | bytes 589824 | tf_op jit(solution)/shard_map/all_to_all | solution.py:279
  833.5 22.8 %reduce-scatter.21.cloned.1.call-done = bf16[768,192]{0,1:T(8,128)(2,1)} async-done(((bf16[3072,192]{0,1:T(8,128)(2,1)}), bf16[768,192]{0,1:T(8,128)(2,1)}) %reduce-scatter.21.cloned.1.call-update) | async-done | bytes 294928 | tf_op jit(solution)/shard_map/reduce_scatter | solution.py:296
  856.3 21.5 %reduce-scatter.19.cloned.1.call-done = bf16[192,192]{1,0:T(8,128)(2,1)} async-done(((bf16[768,192]{1,0:T(8,128)(2,1)}), bf16[192,192]{1,0:T(8,128)(2,1)}) %reduce-scatter.19.cloned.1.call-update) | async-done | bytes 73744 | tf_op jit(solution)/shard_map/reduce_scatter | solution.py:293
  877.9 5.8 convolution_convert_fusion
  893.4 39.6 %all-reduce.1 = (f32[12,128]{1,0:T(8,128)S(1)}, f32[6,768]{1,0:T(8,128)S(1)}, f32[3072]{0:T(1024)S(1)}) all-reduce(f32[12,128]{1,0:T(8,128)S(1)} %dynamic_update_slice.26, f32[6,768]{1,0:T(8,128)S(1)} %dynamic_update_slice.27, f32[3072]{0:T(1024)S(1)} %dynamic_update_slice.28), channel_id=1, replica_groups=mesh['dp'=2,'row'=4,'col'=4] {'dp','row','col'}, use_global_device_ids=true, to_apply=%region_30.31 | all-reduce | flops 9216 | bytes 73728 | tf_op jit(solution)/shard_map/psum | solution.py:328
  942.1 17.5 %reduce-scatter.15.cloned.1.call-done = bf16[2088,192]{0,1:T(8,128)(2,1)} async-done(((bf16[2088,768]{0,1:T(8,128)(2,1)}), bf16[2088,192]{0,1:T(8,128)(2,1)}) %reduce-scatter.15.cloned.1.call-update) | async-done | bytes 801808 | tf_op jit(solution)/shard_map/reduce_scatter | solution.py:26
  (285 shorter events, 122.0 us)
Async XLA Ops:
  7.2 45.4 %all-gather.24.cloned.1.call-start = ((), (), s32[]{:S(2)}) async-start(), calls=%async_computation.25 | async-start | bytes 1671168 | tf_op jit(solution)/shard_map/all_gather | solution.py:176
  7.9 74.6 %all-gather.14.cloned.1.call-start = ((), (), s32[]{:S(2)}) async-start(), calls=%async_computation.12 | async-start | bytes 4177920 | tf_op jit(solution)/shard_map/all_gather | solution.py:12
  8.7 4.6 copy-start.30
  9.0 5.5 copy-start.51
  13.3 125.2 %all-gather.16.cloned.1.call-start = ((), (), s32[]{:S(2)}) async-start(), calls=%async_computation.13 | async-start | bytes 5013504 | tf_op jit(solution)/shard_map/all_gather | solution.py:175
  14.4 245.5 %reduce-scatter.9.cloned.1.call-start = ((), (), s32[]{:S(2)}) async-start(), calls=%async_computation.14 | async-start | bytes 4177920 | tf_op jit(solution)/shard_map/reduce_scatter | solution.py:20
  155.9 4.7 copy-start.24
  179.0 7.8 copy-start.31
  179.0 8.4 copy-start.35
  204.5 7.8 copy-start.31
  204.5 8.4 copy-start.35
  212.9 5.1 copy-start.3
  212.9 9.1 copy-start.5
  222.0 37.9 %copy-start.1 = (bf16[2088,192]{0,1:T(8,128)(2,1)S(1)}, bf16[2088,192]{0,1:T(8,128)(2,1)}, u32[]{:S(2)}) copy-start(bf16[2088,192]{0,1:T(8,128)(2,1)} %reshape.236) | copy-start | bytes 2405380
  222.0 37.9 %copy-start.40 = (f32[192]{0:T(256)S(1)}, f32[192]{0:T(256)}, u32[]{:S(2)}) copy-start(f32[192]{0:T(256)} %param.29) | copy-start | bytes 2308
  222.1 49.8 %copy-start.43 = (f32[192]{0:T(256)S(1)}, f32[192]{0:T(256)}, u32[]{:S(2)}) copy-start(f32[192]{0:T(256)} %param.30) | copy-start | bytes 2308
  222.1 49.8 %copy-start.45 = (f32[192]{0:T(256)S(1)}, f32[192]{0:T(256)}, u32[]{:S(2)}) copy-start(f32[192]{0:T(256)} %param.31) | copy-start | bytes 2308
  222.1 52.5 %copy-start.49 = (f32[768]{0:T(1024)S(1)}, f32[768]{0:T(1024)}, u32[]{:S(2)}) copy-start(f32[768]{0:T(1024)} %param.33) | copy-start | bytes 9220
  222.1 93.4 %all-gather.26.cloned.1.call-start = ((), (), s32[]{:S(2)}) async-start(), calls=%async_computation.26 | async-start | bytes 5013504 | tf_op jit(solution)/shard_map/all_gather | solution.py:177
  222.7 146.7 %all-gather.28.cloned.1.call-start = ((), (), s32[]{:S(2)}) async-start(), calls=%async_computation.27 | async-start | bytes 5013504 | tf_op jit(solution)/shard_map/all_gather | solution.py:178
  223.3 176.3 %all-gather.18.cloned.1.call-start = ((), (), s32[]{:S(2)}) async-start(), calls=%async_computation.15 | async-start | bytes 4177920 | tf_op jit(solution)/shard_map/all_gather | solution.py:12
  271.9 345.0 %copy-start.26 = (f32[2088]{0:T(1024)}, f32[2088]{0:T(1024)S(1)}, u32[]{:S(2)}) copy-start(f32[2088]{0:T(1024)S(1)} %get-tuple-element.235) | copy-start | bytes 25060
  271.9 345.0 %copy-start.28 = (f32[2088]{0:T(1024)}, f32[2088]{0:T(1024)S(1)}, u32[]{:S(2)}) copy-start(f32[2088]{0:T(1024)S(1)} %get-tuple-element.236) | copy-start | bytes 25060
  274.6 191.9 %reduce-scatter.11.cloned.1.call-start = ((), (), s32[]{:S(2)}) async-start(), calls=%async_computation.16 | async-start | bytes 4177920 | tf_op jit(solution)/shard_map/reduce_scatter | solution.py:20
  427.1 39.3 %copy-start.8 = (bf16[2088,192]{0,1:T(8,128)(2,1)S(1)}, bf16[2088,192]{0,1:T(8,128)(2,1)}, u32[]{:S(2)}) copy-start(bf16[2088,192]{0,1:T(8,128)(2,1)} %reduce-scatter.9.cloned.1.call-done) | copy-start | bytes 2405380
  427.1 39.3 %copy-start.52 = (f32[192]{0:T(256)S(1)}, f32[192]{0:T(256)}, u32[]{:S(2)}) copy-start(f32[192]{0:T(256)} %param.35) | copy-start | bytes 2308
  427.1 52.2 %copy-start.42 = (f32[192]{0:T(256)S(1)}, f32[192]{0:T(256)}, u32[]{:S(2)}) copy-start(f32[192]{0:T(256)} %param.36) | copy-start | bytes 2308
  427.1 52.2 %copy-start.53 = (f32[192]{0:T(256)S(1)}, f32[192]{0:T(256)}, u32[]{:S(2)}) copy-start(f32[192]{0:T(256)} %param.37) | copy-start | bytes 2308
  427.2 116.8 %all-gather.20.cloned.1.call-start = ((), (), s32[]{:S(2)}) async-start(), calls=%async_computation.17 | async-start | bytes 4177920 | tf_op jit(solution)/shard_map/all_gather | solution.py:16
  513.6 87.9 %reduce-scatter.13.cloned.1.call-start = ((), (), s32[]{:S(2)}) async-start(), calls=%async_computation.18 | async-start | bytes 4177920 | tf_op jit(solution)/shard_map/reduce_scatter | solution.py:26
  562.2 88.1 %all-gather.22.cloned.1.call-start = ((), (), s32[]{:S(2)}) async-start(), calls=%async_computation.19 | async-start | bytes 4177920 | tf_op jit(solution)/shard_map/all_gather | solution.py:16
  616.8 37.3 %copy-start.36 = (f32[2088]{0:T(1024)}, f32[2088]{0:T(1024)S(1)}, u32[]{:S(2)}) copy-start(f32[2088]{0:T(1024)S(1)} %broadcast_multiply_fusion) | copy-start | bytes 25060
  616.8 37.3 %copy-start.38 = (f32[2088]{0:T(1024)}, f32[2088]{0:T(1024)S(1)}, u32[]{:S(2)}) copy-start(f32[2088]{0:T(1024)S(1)} %broadcast_multiply_fusion.1) | copy-start | bytes 25060
  620.0 211.4 %reduce-scatter.17.cloned.1.call-start = ((), (), s32[]{:S(2)}) async-start(), calls=%async_computation.21 | async-start | bytes 1474560 | tf_op jit(solution)/shard_map/reduce_scatter | solution.py:290
  654.1 6.8 copy-start.4
  654.1 6.8 copy-start.6
  654.1 6.8 copy-start.33
  673.5 8.6 copy-start.7
  682.0 8.3 copy-start
  682.0 8.3 copy-start.17
  707.5 8.6 copy-start.7
  716.0 8.3 copy-start
  716.0 8.3 copy-start.17
  766.5 67.0 %reduce-scatter.23.cloned.1.call-start = ((), (), s32[]{:S(2)}) async-start(), calls=%async_computation.24 | async-start | bytes 1474560 | tf_op jit(solution)/shard_map/reduce_scatter | solution.py:299
  772.4 19.8 %copy-start.22 = (bf16[2088,768]{1,0:T(8,128)(2,1)S(1)}, bf16[2088,768]{1,0:T(8,128)(2,1)}, u32[]{:S(2)}) copy-start(bf16[2088,768]{1,0:T(8,128)(2,1)} %copy-done.21) | copy-start | bytes 9621508
  792.2 64.2 %reduce-scatter.21.cloned.1.call-start = ((), (), s32[]{:S(2)}) async-start(), calls=%async_computation.23 | async-start | bytes 1474560 | tf_op jit(solution)/shard_map/reduce_scatter | solution.py:296
  797.1 20.1 %copy-start.13 = (bf16[2088,192]{0,1:T(8,128)(2,1)S(1)}, bf16[2088,192]{0,1:T(8,128)(2,1)}, u32[]{:S(2)}) copy-start(bf16[2088,192]{0,1:T(8,128)(2,1)} %copy-done.12) | copy-start | bytes 2405380
  816.7 61.1 %reduce-scatter.19.cloned.1.call-start = ((), (), s32[]{:S(2)}) async-start(), calls=%async_computation.22 | async-start | bytes 491520 | tf_op jit(solution)/shard_map/reduce_scatter | solution.py:293
  820.3 57.6 %copy-start.15 = (bf16[2088,576]{0,1:T(8,128)(2,1)S(1)}, bf16[2088,576]{0,1:T(8,128)(2,1)}, u32[]{:S(2)}) copy-start(bf16[2088,576]{0,1:T(8,128)(2,1)} %reshape.250) | copy-start | bytes 7216132
  831.4 103.6 %all-reduce.9.cloned.1.call-start = ((), (), s32[]{:S(2)}) async-start(), calls=%async_computation.28 | async-start | bytes 1966080 | tf_op jit(solution)/shard_map/psum | solution.py:304
  877.9 81.7 %reduce-scatter.15.cloned.1.call-start = ((), (), s32[]{:S(2)}) async-start(), calls=%async_computation.20 | async-start | bytes 4177920 | tf_op jit(solution)/shard_map/reduce_scatter | solution.py:26
  885.5 4.8 copy-start.46
  885.5 4.8 copy-start.47
  885.5 4.9 copy-start.48
  885.5 4.9 copy-start.50
  888.6 70.9 %copy-start.2 = (bf16[2088,192]{0,1:T(8,128)(2,1)S(1)}, bf16[2088,192]{0,1:T(8,128)(2,1)}, u32[]{:S(2)}) copy-start(bf16[2088,192]{0,1:T(8,128)(2,1)} %reshape.236) | copy-start | bytes 2405380
  888.6 70.9 %copy-start.9 = (bf16[2088,192]{0,1:T(8,128)(2,1)S(1)}, bf16[2088,192]{0,1:T(8,128)(2,1)}, u32[]{:S(2)}) copy-start(bf16[2088,192]{0,1:T(8,128)(2,1)} %reduce-scatter.9.cloned.1.call-done) | copy-start | bytes 2405380
  888.6 70.9 %copy-start.11 = (f32[2088,192]{0,1:T(8,128)S(1)}, f32[2088,192]{0,1:T(8,128)}, u32[]{:S(2)}) copy-start(f32[2088,192]{0,1:T(8,128)} %get-tuple-element.213) | copy-start | bytes 4810756
  888.6 70.9 %copy-start.27 = (f32[2088]{0:T(1024)S(1)}, f32[2088]{0:T(1024)}, u32[]{:S(2)}) copy-start(f32[2088]{0:T(1024)} %copy-done.26) | copy-start | bytes 25060
  888.6 70.9 %copy-start.29 = (f32[2088]{0:T(1024)S(1)}, f32[2088]{0:T(1024)}, u32[]{:S(2)}) copy-start(f32[2088]{0:T(1024)} %copy-done.28) | copy-start | bytes 25060
  888.6 70.9 %copy-start.37 = (f32[2088]{0:T(1024)S(1)}, f32[2088]{0:T(1024)}, u32[]{:S(2)}) copy-start(f32[2088]{0:T(1024)} %copy-done.36) | copy-start | bytes 25060
  888.7 70.9 %copy-start.39 = (f32[2088]{0:T(1024)S(1)}, f32[2088]{0:T(1024)}, u32[]{:S(2)}) copy-start(f32[2088]{0:T(1024)} %copy-done.38) | copy-start | bytes 25060
  888.7 70.9 %copy-start.41 = (f32[192]{0:T(256)S(1)}, f32[192]{0:T(256)}, u32[]{:S(2)}) copy-start(f32[192]{0:T(256)} %param.29) | copy-start | bytes 2308
  888.7 70.9 %copy-start.44 = (f32[192]{0:T(256)S(1)}, f32[192]{0:T(256)}, u32[]{:S(2)}) copy-start(f32[192]{0:T(256)} %param.30) | copy-start | bytes 2308
  (19 other events, 30.9 us)
Sparse Core Ops, SparseCore 0:
  10.3 42.2 all-gather.23
  54.2 28.3 all-gather.13
  85.4 53.1 all-gather.15
  222.2 37.6 reduce-scatter.8
  262.0 53.4 all-gather.25
  317.6 51.7 all-gather.27
  371.5 27.9 all-gather.17
  427.3 39.0 reduce-scatter.10
  513.7 30.2 all-gather.19
  562.3 39.1 reduce-scatter.12
  620.2 30.1 all-gather.21
  766.6 29.3 reduce-scatter.16
  798.3 27.9 reduce-scatter.22
  828.4 27.9 reduce-scatter.20
  858.5 19.3 reduce-scatter.18
  880.8 37.2 all-reduce.8
  920.5 39.0 reduce-scatter.14
where the time goes:
time: 987 us; the launch traced here: 977 us
  waiting for transfers between devices  413 us (42%)
  blocking collectives  178 us (18%)
  matrix products  162 us (16%)
  local copies, waits for them, and re-layouts  134 us (14%)
  other arithmetic  71.6 us (7%)
  between operations  15.7 us (2%)
    reduce_scatter x2, waiting for transfers between devices, forward_reduce(): lax.psum_scatter(partial_rows.astype(jnp.bfloat16), 'col', scatter_dimens...  73.6 us
    all_gather x2, waiting for transfers between devices, back_gather(): return lax.all_gather(shard, 'col', axis=1, tiled=True)  60 us
    reduce_scatter x2, waiting for transfers between devices, backward_reduce(): lax.psum_scatter(partial_rows.astype(jnp.bfloat16), 'col', scatter_dimens...  56.7 us
    all_gather x1, waiting for transfers between devices, per_device(): lax.all_gather(qkv_blocks[None], ('row', 'col'), axis=0, tiled=True)  47.3 us
    dot_general x4, matrix products, against(): lax.dot_general(piece_rows, matrix, (((1,), (1,)), ((), ())), preferred_e...  40 us
    psum x1, blocking collectives, per_device(): lax.psum((heads_pad, units_pad, feat_pad), ('dp', 'row', 'col'))  39.6 us
    all_gather x2, waiting for transfers between devices, gather_feats(): return lax.all_gather(shard, 'col', axis=1, tiled=True)  39.1 us
    all_gather x1, waiting for transfers between devices, per_device(): lax.all_gather(down_blocks[None], ('row', 'col'), axis=0, tiled=True)  38.2 us
  transfers between devices with their start and end apart: 17, of which 14 were waited for; matrix products, arithmetic and copies ran while one was open for 10% of the time, Pallas kernels for 0%

commit v1 on v0

--- a/solution.py
+++ b/solution.py
@@ -273,8 +273,14 @@
     )
     grad_in = grad_one + backward_reduce(against(grad_proj, flat_qkv))
     relayed = (
-        lax.all_to_all(
-            grad_heads.astype(jnp.bfloat16), "col", split_axis=1, concat_axis=0, tiled=True
+        jnp.concatenate(
+            lax.all_to_all(
+                jnp.stack(jnp.split(grad_heads.astype(jnp.bfloat16), lax.axis_size("col"), axis=1)),
+                "col",
+                0,
+                0,
+            ),
+            axis=0,
         ).astype(grad_heads.dtype),
         lax.all_to_all(
             grad_out_rows.astype(jnp.bfloat16), "col", split_axis=1, concat_axis=0, tiled=True

time: 987 us -> 982 us (level)
  no operation moved by 1% of the time
where the time goes in v1:
time: 982 us; the launch traced here: 972 us
  waiting for transfers between devices  415 us (42%)
  blocking collectives  174 us (18%)
  matrix products  162 us (16%)
  local copies, waits for them, and re-layouts  131 us (13%)
  other arithmetic  71.8 us (7%)
  between operations  15.7 us (2%)
    reduce_scatter x2, waiting for transfers between devices, forward_reduce(): lax.psum_scatter(partial_rows.astype(jnp.bfloat16), 'col', scatter_dimens...  73.6 us
    all_gather x2, waiting for transfers between devices, back_gather(): return lax.all_gather(shard, 'col', axis=1, tiled=True)  60 us
    reduce_scatter x2, waiting for transfers between devices, backward_reduce(): lax.psum_scatter(partial_rows.astype(jnp.bfloat16), 'col', scatter_dimens...  56.7 us
    all_gather x1, waiting for transfers between devices, per_device(): lax.all_gather(qkv_blocks[None], ('row', 'col'), axis=0, tiled=True)  47.3 us
    dot_general x4, matrix products, against(): lax.dot_general(piece_rows, matrix, (((1,), (1,)), ((), ())), preferred_e...  40.1 us
    psum x1, blocking collectives, per_device(): lax.psum((heads_pad, units_pad, feat_pad), ('dp', 'row', 'col'))  39.6 us
    all_gather x2, waiting for transfers between devices, gather_feats(): return lax.all_gather(shard, 'col', axis=1, tiled=True)  39.1 us
    all_gather x1, waiting for transfers between devices, per_device(): lax.all_gather(down_blocks[None], ('row', 'col'), axis=0, tiled=True)  38.2 us
  transfers between devices with their start and end apart: 17, of which 14 were waited for; matrix products, arithmetic and copies ran while one was open for 10% of the time, Pallas kernels for 0%

profile of v1, /device:TPU:0, one launch (start us, length us, event | category | flops | bytes accessed | tf_op | source)
XLA Modules:
  0.0 971.9 jit_solution(12186899716325460008)
XLA Ops:
  14.5 13.6 %all-gather.3 = f32[4,3,128]{2,1,0:T(4,128)S(1)} all-gather(f32[1,3,128]{2,1,0:T(4,128)S(1)} %bitcast.269), channel_id=1, replica_groups=mesh['dp'=2,'row'=4,'col'=4] {'row'}, dimensions={0}, use_global_device_ids=true | all-gather | bytes 7680 | tf_op jit(solution)/shard_map/all_gather | solution.py:191
  28.2 24.4 %all-gather.24.cloned.1.call-done = bf16[3072,192]{1,0:T(8,128)(2,1)} async-done(((bf16[192,192]{1,0:T(8,128)(2,1)}), bf16[3072,192]{1,0:T(8,128)(2,1)}) %all-gather.24.cloned.1.call-update) | async-done | bytes 1179664 | tf_op jit(solution)/shard_map/all_gather | solution.py:176
  57.5 25.0 %all-gather.14.cloned.1.call-done = bf16[2088,768]{0,1:T(8,128)(2,1)} async-done(((bf16[2088,192]{0,1:T(8,128)(2,1)}), bf16[2088,768]{0,1:T(8,128)(2,1)}) %all-gather.14.cloned.1.call-update) | async-done | bytes 3207184 | tf_op jit(solution)/shard_map/all_gather | solution.py:12
  82.5 8.7 reshape.279
  91.2 47.3 %all-gather.16.cloned.1.call-done = bf16[16,3,192,192]{3,2,1,0:T(8,128)(2,1)} async-done(((bf16[1,3,192,192]{3,2,1,0:T(8,128)(2,1)}), bf16[16,3,192,192]{3,2,1,0:T(8,128)(2,1)}) %all-gather.16.cloned.1.call-update) | async-done | bytes 3538960 | tf_op jit(solution)/shard_map/all_gather | solution.py:175
  138.5 9.7 copy.109
  148.2 7.7 reshape.241
  156.0 4.7 fusion.60
  161.5 51.5 %while.26 = (s32[]{:T(128)}, bf16[2,1044,3,64]{1,3,2,0:T(8,128)(2,1)S(1)}, f32[2,3,1044]{2,1,0:T(4,128)}, bf16[2,1044,3,64]{1,3,2,0:T(8,128)(2,1)S(1)}, s32[2,10...) while((s32[]{:T(128)}, ...), condition=%wide.region_3.4_spmd, body=%wide.region_0.3_spmd.sunk | while | flops 864516608 | bytes 43690424 | solution.py:208
  163.9 8.0 fusion.151
  171.9 7.1 fusion.152
  179.0 7.8 fusion.153
  189.5 8.0 fusion.151
  197.4 7.1 fusion.152
  204.5 7.8 fusion.153
  218.1 4.0 convolution_convert_fusion.3
  223.5 36.4 %reduce-scatter.9.cloned.1.call-done = bf16[2088,192]{0,1:T(8,128)(2,1)} async-done(((bf16[2088,768]{0,1:T(8,128)(2,1)}), bf16[2088,192]{0,1:T(8,128)(2,1)}) %reduce-scatter.9.cloned.1.call-update) | async-done | bytes 801808 | tf_op jit(solution)/shard_map/reduce_scatter | solution.py:20
  261.6 10.3 %all-reduce.5 = (f32[2088]{0:T(1024)S(1)}, f32[2088]{0:T(1024)S(1)}) all-reduce(f32[2088]{0:T(1024)S(1)} %get-tuple-element.158, f32[2088]{0:T(1024)S(1)} %get-tuple-element.157), channel_id=1, replica_groups=mesh['dp'=2,'row'=4,'col'=4] {'col'}, use_global_device_ids=true, to_apply=%region_8.9 | all-reduce | flops 4176 | bytes 33408 | tf_op jit(solution)/shard_map/psum | solution.py:56
  274.7 13.2 %all-gather.4 = f32[4,1,768]{2,1,0:T(1,128)S(1)} all-gather(f32[1,1,768]{2,1,0:T(1,128)S(1)} %reshape.266), channel_id=1, replica_groups=mesh['dp'=2,'row'=4,'col'=4] {'row'}, dimensions={0}, use_global_device_ids=true | all-gather | bytes 15360 | tf_op jit(solution)/shard_map/all_gather | solution.py:192
  288.0 27.6 %all-gather.26.cloned.1.call-done = bf16[12288,192]{0,1:T(8,128)(2,1)} async-done(((bf16[768,192]{0,1:T(8,128)(2,1)}), bf16[12288,192]{0,1:T(8,128)(2,1)}) %all-gather.26.cloned.1.call-update) | async-done | bytes 4718608 | tf_op jit(solution)/shard_map/all_gather | solution.py:177
  315.6 8.2 reshape.246
  323.8 4.3 copy.112
  328.1 3.2 copy.140
  331.3 38.2 %all-gather.28.cloned.1.call-done = bf16[12288,192]{0,1:T(8,128)(2,1)} async-done(((bf16[768,192]{0,1:T(8,128)(2,1)}), bf16[12288,192]{0,1:T(8,128)(2,1)}) %all-gather.28.cloned.1.call-update) | async-done | bytes 4718608 | tf_op jit(solution)/shard_map/all_gather | solution.py:178
  369.5 8.3 reshape.248
  377.8 4.6 copy.113
  385.6 14.0 %all-gather.18.cloned.1.call-done = bf16[2088,768]{0,1:T(8,128)(2,1)} async-done(((bf16[2088,192]{0,1:T(8,128)(2,1)}), bf16[2088,768]{0,1:T(8,128)(2,1)}) %all-gather.18.cloned.1.call-update) | async-done | bytes 3207184 | tf_op jit(solution)/shard_map/all_gather | solution.py:12
  399.6 20.0 %multiply_convert_fusion.1 = (bf16[2088,768]{1,0:T(8,128)(2,1)S(1)}, f32[2088,768]{1,0:T(8,128)}, f32[2088,768]{1,0:T(8,128)}) fusion(f32[768]{0:T(1024)S(1)} %dynamic_slice.67, bf16[2088,768]{0,1:T(8,128)(2,1)} %all-gather.18.cloned.1.call-done, bf16[3072,768]{0,1:T(8,128)(2,1)} %bitcast.240, s32[]{:T(128)S(6)} %select_n.38), kind=kOutput, calls=%fused_computation.65 | convolution fusion | flops 2568941568 | bytes 20560900 | tf_op jit(solution)/shard_map/dot_general | solution.py:32
  421.3 5.9 convolution_convert_fusion.2
  429.3 37.2 %reduce-scatter.11.cloned.1.call-done = bf16[2088,192]{0,1:T(8,128)(2,1)} async-done(((bf16[2088,768]{0,1:T(8,128)(2,1)}), bf16[2088,192]{0,1:T(8,128)(2,1)}) %reduce-scatter.11.cloned.1.call-update) | async-done | bytes 801808 | tf_op jit(solution)/shard_map/reduce_scatter | solution.py:20
  468.8 10.6 %all-reduce.4 = (f32[2088]{0:T(1024)S(1)}, f32[2088]{0:T(1024)S(1)}) all-reduce(f32[2088]{0:T(1024)S(1)} %get-tuple-element.161, f32[2088]{0:T(1024)S(1)} %get-tuple-element.160), channel_id=1, replica_groups=mesh['dp'=2,'row'=4,'col'=4] {'col'}, use_global_device_ids=true, to_apply=%region_13.14 | all-reduce | flops 4176 | bytes 33408 | tf_op jit(solution)/shard_map/psum | solution.py:56
  481.0 3.5 reshape.250
  490.3 4.5 pad.4.clone
  494.8 3.3 reshape.251
  500.6 10.3 %all-reduce.3 = (f32[2088]{0:T(1024)S(1)}, f32[2088]{0:T(1024)S(1)}) all-reduce(f32[2088]{0:T(1024)S(1)} %get-tuple-element.155, f32[2088]{0:T(1024)S(1)} %reduce_sum.143), channel_id=1, replica_groups=mesh['dp'=2,'row'=4,'col'=4] {'col'}, use_global_device_ids=true, to_apply=%region_18.19 | all-reduce | flops 4176 | bytes 33408 | tf_op jit(solution)/shard_map/psum | solution.py:67
  514.2 29.9 %all-gather.20.cloned.1.call-done = bf16[2088,768]{0,1:T(8,128)(2,1)} async-done(((bf16[2088,192]{0,1:T(8,128)(2,1)}), bf16[2088,768]{0,1:T(8,128)(2,1)}) %all-gather.20.cloned.1.call-update) | async-done | bytes 3207184 | tf_op jit(solution)/shard_map/all_gather | solution.py:16
  544.1 10.5 %add_convert_fusion = bf16[2088,768]{1,0:T(8,128)(2,1)S(1)} fusion(f32[2088,768]{1,0:T(8,128)} %get-tuple-element.216, f32[2088,768]{1,0:T(8,128)} %get-tuple-element.245, bf16[2088,768]{0,1:T(8,128)(2,1)} %all-gather.20.cloned.1.call-done, bf16[3072,768]{0,1:T(8,128)(2,1)} %bitcast.243, s32[]{:T(128)S(6)} %select_n.38), kind=kOutput, calls=%fused_computation.64 | convolution fusion | flops 2485555200 | bytes 20557828 | tf_op jit(solution)/shard_map/dot_general | solution.py:32
  556.3 6.0 convolution_convert_fusion.1
  562.3 39.2 %reduce-scatter.13.cloned.1.call-done = bf16[2088,192]{0,1:T(8,128)(2,1)} async-done(((bf16[2088,768]{0,1:T(8,128)(2,1)}), bf16[2088,192]{0,1:T(8,128)(2,1)}) %reduce-scatter.13.cloned.1.call-update) | async-done | bytes 801808 | tf_op jit(solution)/shard_map/reduce_scatter | solution.py:26
  601.6 5.0 multiply_reduce_fusion.3
  606.6 10.3 %all-reduce.2 = (f32[2088]{0:T(1024)S(1)}, f32[2088]{0:T(1024)S(1)}) all-reduce(f32[2088]{0:T(1024)S(1)} %get-tuple-element.153, f32[2088]{0:T(1024)S(1)} %get-tuple-element.156), channel_id=1, replica_groups=mesh['dp'=2,'row'=4,'col'=4] {'col'}, use_global_device_ids=true, to_apply=%region_23.24 | all-reduce | flops 4176 | bytes 33408 | tf_op jit(solution)/shard_map/psum | solution.py:67
  620.3 30.1 %all-gather.22.cloned.1.call-done = bf16[2088,768]{0,1:T(8,128)(2,1)} async-done(((bf16[2088,192]{0,1:T(8,128)(2,1)}), bf16[2088,768]{0,1:T(8,128)(2,1)}) %all-gather.22.cloned.1.call-update) | async-done | bytes 3207184 | tf_op jit(solution)/shard_map/all_gather | solution.py:16
  650.4 3.7 convolution_convert_fusion.4
  661.0 67.8 %while.27 = (s32[]{:T(128)}, bf16[2,1044,3,64]{1,3,2,0:T(8,128)(2,1)}, bf16[2,1044,3,64]{1,3,2,0:T(8,128)(2,1)}, bf16[2,1044,3,64]{1,3,2,0:T(8,128)(2,1)}, bf16[...) while((s32[]{:T(128)}, ...), condition=%wide.region_26.27_spmd, body=%wide.region_24.26_spmd.sunk | while | flops 2124194560 | bytes 151329200 | solution.py:262
  661.9 3.4 fusion.162
  665.3 8.0 multiply_reduce_fusion.10
  673.4 8.6 multiply_convert_fusion.3
  681.9 8.3 fusion.165
  695.7 3.4 fusion.162
  699.1 8.0 multiply_reduce_fusion.10
  707.2 8.6 multiply_convert_fusion.3
  715.7 8.3 fusion.165
  736.4 5.0 fusion.72
  742.0 19.1 %all_to_all.62 = bf16[4,3,192,192]{2,3,1,0:T(8,128)(2,1)} all-to-all(bf16[4,3,192,192]{2,3,1,0:T(8,128)(2,1)S(1)} %pad_maximum_fusion.1), channel_id=1, replica_groups=mesh['dp'=2,'row'=4,'col'=4] {'col'}, dimensions={0} | all-to-all | bytes 1769472 | tf_op jit(solution)/shard_map/all_to_all | solution.py:277
  761.2 4.8 convolution_convert_fusion.5
  766.1 18.5 %all_to_all.63 = bf16[768,4,192]{0,2,1:T(8,128)(2,1)S(1)} all-to-all(bf16[768,4,192]{0,2,1:T(8,128)(2,1)S(1)} %bitcast.253), channel_id=1, replica_groups=mesh['dp'=2,'row'=4,'col'=4] {'col'}, dimensions={1} | all-to-all | bytes 2359296 | tf_op jit(solution)/shard_map/all_to_all | solution.py:291
  785.9 4.9 convolution_convert_fusion.6
  790.7 18.4 %all_to_all.64 = bf16[768,4,192]{0,2,1:T(8,128)(2,1)S(1)} all-to-all(bf16[768,4,192]{0,2,1:T(8,128)(2,1)S(1)} %bitcast.254), channel_id=1, replica_groups=mesh['dp'=2,'row'=4,'col'=4] {'col'}, dimensions={1} | all-to-all | bytes 2359296 | tf_op jit(solution)/shard_map/all_to_all | solution.py:288
  814.3 10.6 %all_to_all.65 = bf16[192,4,192]{2,0,1:T(8,128)(2,1)} all-to-all(bf16[192,4,192]{2,0,1:T(8,128)(2,1)S(1)} %copy.123), channel_id=1, replica_groups=mesh['dp'=2,'row'=4,'col'=4] {'col'}, dimensions={1} | all-to-all | bytes 589824 | tf_op jit(solution)/shard_map/all_to_all | solution.py:285
  827.3 24.3 %reduce-scatter.21.cloned.1.call-done = bf16[768,192]{0,1:T(8,128)(2,1)} async-done(((bf16[3072,192]{0,1:T(8,128)(2,1)}), bf16[768,192]{0,1:T(8,128)(2,1)}) %reduce-scatter.21.cloned.1.call-update) | async-done | bytes 294928 | tf_op jit(solution)/shard_map/reduce_scatter | solution.py:302
  851.6 21.6 %reduce-scatter.19.cloned.1.call-done = bf16[192,192]{1,0:T(8,128)(2,1)} async-done(((bf16[768,192]{1,0:T(8,128)(2,1)}), bf16[192,192]{1,0:T(8,128)(2,1)}) %reduce-scatter.19.cloned.1.call-update) | async-done | bytes 73744 | tf_op jit(solution)/shard_map/reduce_scatter | solution.py:299
  873.2 5.8 convolution_convert_fusion
  888.7 39.6 %all-reduce.1 = (f32[12,128]{1,0:T(8,128)S(1)}, f32[6,768]{1,0:T(8,128)S(1)}, f32[3072]{0:T(1024)S(1)}) all-reduce(f32[12,128]{1,0:T(8,128)S(1)} %dynamic_update_slice.26, f32[6,768]{1,0:T(8,128)S(1)} %dynamic_update_slice.27, f32[3072]{0:T(1024)S(1)} %dynamic_update_slice.28), channel_id=1, replica_groups=mesh['dp'=2,'row'=4,'col'=4] {'dp','row','col'}, use_global_device_ids=true, to_apply=%region_30.31 | all-reduce | flops 9216 | bytes 73728 | tf_op jit(solution)/shard_map/psum | solution.py:334
  937.3 17.5 %reduce-scatter.15.cloned.1.call-done = bf16[2088,192]{0,1:T(8,128)(2,1)} async-done(((bf16[2088,768]{0,1:T(8,128)(2,1)}), bf16[2088,192]{0,1:T(8,128)(2,1)}) %reduce-scatter.15.cloned.1.call-update) | async-done | bytes 801808 | tf_op jit(solution)/shard_map/reduce_scatter | solution.py:26
  (286 shorter events, 119.4 us)
Async XLA Ops:
  7.2 45.4 %all-gather.24.cloned.1.call-start = ((), (), s32[]{:S(2)}) async-start(), calls=%async_computation.25 | async-start | bytes 1671168 | tf_op jit(solution)/shard_map/all_gather | solution.py:176
  7.9 74.6 %all-gather.14.cloned.1.call-start = ((), (), s32[]{:S(2)}) async-start(), calls=%async_computation.12 | async-start | bytes 4177920 | tf_op jit(solution)/shard_map/all_gather | solution.py:12
  9.0 5.5 copy-start.51
  13.3 125.2 %all-gather.16.cloned.1.call-start = ((), (), s32[]{:S(2)}) async-start(), calls=%async_computation.13 | async-start | bytes 5013504 | tf_op jit(solution)/shard_map/all_gather | solution.py:175
  14.4 245.5 %reduce-scatter.9.cloned.1.call-start = ((), (), s32[]{:S(2)}) async-start(), calls=%async_computation.14 | async-start | bytes 4177920 | tf_op jit(solution)/shard_map/reduce_scatter | solution.py:20
  155.9 4.7 copy-start.24
  179.0 7.8 copy-start.31
  179.0 8.4 copy-start.35
  204.5 7.8 copy-start.31
  204.5 8.4 copy-start.35
  213.0 5.1 copy-start.3
  213.0 9.1 copy-start.5
  222.1 37.9 %copy-start.1 = (bf16[2088,192]{0,1:T(8,128)(2,1)S(1)}, bf16[2088,192]{0,1:T(8,128)(2,1)}, u32[]{:S(2)}) copy-start(bf16[2088,192]{0,1:T(8,128)(2,1)} %reshape.239) | copy-start | bytes 2405380
  222.1 37.9 %copy-start.40 = (f32[192]{0:T(256)S(1)}, f32[192]{0:T(256)}, u32[]{:S(2)}) copy-start(f32[192]{0:T(256)} %param.29) | copy-start | bytes 2308
  222.1 49.8 %copy-start.43 = (f32[192]{0:T(256)S(1)}, f32[192]{0:T(256)}, u32[]{:S(2)}) copy-start(f32[192]{0:T(256)} %param.30) | copy-start | bytes 2308
  222.1 49.8 %copy-start.45 = (f32[192]{0:T(256)S(1)}, f32[192]{0:T(256)}, u32[]{:S(2)}) copy-start(f32[192]{0:T(256)} %param.31) | copy-start | bytes 2308
  222.1 52.5 %copy-start.49 = (f32[768]{0:T(1024)S(1)}, f32[768]{0:T(1024)}, u32[]{:S(2)}) copy-start(f32[768]{0:T(1024)} %param.33) | copy-start | bytes 9220
  222.1 93.4 %all-gather.26.cloned.1.call-start = ((), (), s32[]{:S(2)}) async-start(), calls=%async_computation.26 | async-start | bytes 5013504 | tf_op jit(solution)/shard_map/all_gather | solution.py:177
  222.7 146.7 %all-gather.28.cloned.1.call-start = ((), (), s32[]{:S(2)}) async-start(), calls=%async_computation.27 | async-start | bytes 5013504 | tf_op jit(solution)/shard_map/all_gather | solution.py:178
  223.3 176.3 %all-gather.18.cloned.1.call-start = ((), (), s32[]{:S(2)}) async-start(), calls=%async_computation.15 | async-start | bytes 4177920 | tf_op jit(solution)/shard_map/all_gather | solution.py:12
  271.9 345.0 %copy-start.26 = (f32[2088]{0:T(1024)}, f32[2088]{0:T(1024)S(1)}, u32[]{:S(2)}) copy-start(f32[2088]{0:T(1024)S(1)} %get-tuple-element.239) | copy-start | bytes 25060
  271.9 345.0 %copy-start.28 = (f32[2088]{0:T(1024)}, f32[2088]{0:T(1024)S(1)}, u32[]{:S(2)}) copy-start(f32[2088]{0:T(1024)S(1)} %get-tuple-element.240) | copy-start | bytes 25060
  274.6 191.9 %reduce-scatter.11.cloned.1.call-start = ((), (), s32[]{:S(2)}) async-start(), calls=%async_computation.16 | async-start | bytes 4177920 | tf_op jit(solution)/shard_map/reduce_scatter | solution.py:20
  427.2 39.3 %copy-start.8 = (bf16[2088,192]{0,1:T(8,128)(2,1)S(1)}, bf16[2088,192]{0,1:T(8,128)(2,1)}, u32[]{:S(2)}) copy-start(bf16[2088,192]{0,1:T(8,128)(2,1)} %reduce-scatter.9.cloned.1.call-done) | copy-start | bytes 2405380
  427.2 39.3 %copy-start.52 = (f32[192]{0:T(256)S(1)}, f32[192]{0:T(256)}, u32[]{:S(2)}) copy-start(f32[192]{0:T(256)} %param.35) | copy-start | bytes 2308
  427.2 52.2 %copy-start.42 = (f32[192]{0:T(256)S(1)}, f32[192]{0:T(256)}, u32[]{:S(2)}) copy-start(f32[192]{0:T(256)} %param.36) | copy-start | bytes 2308
  427.2 52.2 %copy-start.53 = (f32[192]{0:T(256)S(1)}, f32[192]{0:T(256)}, u32[]{:S(2)}) copy-start(f32[192]{0:T(256)} %param.37) | copy-start | bytes 2308
  427.2 116.8 %all-gather.20.cloned.1.call-start = ((), (), s32[]{:S(2)}) async-start(), calls=%async_computation.17 | async-start | bytes 4177920 | tf_op jit(solution)/shard_map/all_gather | solution.py:16
  513.6 87.9 %reduce-scatter.13.cloned.1.call-start = ((), (), s32[]{:S(2)}) async-start(), calls=%async_computation.18 | async-start | bytes 4177920 | tf_op jit(solution)/shard_map/reduce_scatter | solution.py:26
  562.3 88.1 %all-gather.22.cloned.1.call-start = ((), (), s32[]{:S(2)}) async-start(), calls=%async_computation.19 | async-start | bytes 4177920 | tf_op jit(solution)/shard_map/all_gather | solution.py:16
  616.9 37.3 %copy-start.36 = (f32[2088]{0:T(1024)}, f32[2088]{0:T(1024)S(1)}, u32[]{:S(2)}) copy-start(f32[2088]{0:T(1024)S(1)} %broadcast_multiply_fusion) | copy-start | bytes 25060
  616.9 37.3 %copy-start.38 = (f32[2088]{0:T(1024)}, f32[2088]{0:T(1024)S(1)}, u32[]{:S(2)}) copy-start(f32[2088]{0:T(1024)S(1)} %broadcast_multiply_fusion.1) | copy-start | bytes 25060
  620.1 204.9 %reduce-scatter.17.cloned.1.call-start = ((), (), s32[]{:S(2)}) async-start(), calls=%async_computation.21 | async-start | bytes 1474560 | tf_op jit(solution)/shard_map/reduce_scatter | solution.py:296
  654.2 6.8 copy-start.4
  654.2 6.8 copy-start.6
  654.2 6.8 copy-start.33
  673.4 8.6 copy-start.7
  681.9 8.3 copy-start
  681.9 8.3 copy-start.17
  707.2 8.6 copy-start.7
  715.7 8.3 copy-start
  715.7 8.3 copy-start.17
  741.7 19.5 %copy-start.54 = (bf16[2088,768]{0,1:T(8,128)(2,1)S(1)}, bf16[2088,768]{0,1:T(8,128)(2,1)}, u32[]{:S(2)}) copy-start(bf16[2088,768]{0,1:T(8,128)(2,1)} %all-gather.20.cloned.1.call-done) | copy-start | bytes 9621508
  761.2 66.1 %reduce-scatter.23.cloned.1.call-start = ((), (), s32[]{:S(2)}) async-start(), calls=%async_computation.24 | async-start | bytes 1474560 | tf_op jit(solution)/shard_map/reduce_scatter | solution.py:305
  766.1 19.8 %copy-start.22 = (bf16[2088,768]{1,0:T(8,128)(2,1)S(1)}, bf16[2088,768]{1,0:T(8,128)(2,1)}, u32[]{:S(2)}) copy-start(bf16[2088,768]{1,0:T(8,128)(2,1)} %copy-done.21) | copy-start | bytes 9621508
  785.8 65.8 %reduce-scatter.21.cloned.1.call-start = ((), (), s32[]{:S(2)}) async-start(), calls=%async_computation.23 | async-start | bytes 1474560 | tf_op jit(solution)/shard_map/reduce_scatter | solution.py:302
  790.7 20.0 %copy-start.13 = (bf16[2088,192]{0,1:T(8,128)(2,1)S(1)}, bf16[2088,192]{0,1:T(8,128)(2,1)}, u32[]{:S(2)}) copy-start(bf16[2088,192]{0,1:T(8,128)(2,1)} %copy-done.12) | copy-start | bytes 2405380
  810.3 62.8 %reduce-scatter.19.cloned.1.call-start = ((), (), s32[]{:S(2)}) async-start(), calls=%async_computation.22 | async-start | bytes 491520 | tf_op jit(solution)/shard_map/reduce_scatter | solution.py:299
  813.9 59.3 %copy-start.15 = (bf16[2088,576]{0,1:T(8,128)(2,1)S(1)}, bf16[2088,576]{0,1:T(8,128)(2,1)}, u32[]{:S(2)}) copy-start(bf16[2088,576]{0,1:T(8,128)(2,1)} %reshape.253) | copy-start | bytes 7216132
  825.0 105.2 %all-reduce.9.cloned.1.call-start = ((), (), s32[]{:S(2)}) async-start(), calls=%async_computation.28 | async-start | bytes 1966080 | tf_op jit(solution)/shard_map/psum | solution.py:310
  873.2 81.6 %reduce-scatter.15.cloned.1.call-start = ((), (), s32[]{:S(2)}) async-start(), calls=%async_computation.20 | async-start | bytes 4177920 | tf_op jit(solution)/shard_map/reduce_scatter | solution.py:26
  880.8 4.8 copy-start.46
  880.8 4.8 copy-start.47
  880.8 4.9 copy-start.48
  880.8 4.9 copy-start.50
  883.9 70.9 %copy-start.2 = (bf16[2088,192]{0,1:T(8,128)(2,1)S(1)}, bf16[2088,192]{0,1:T(8,128)(2,1)}, u32[]{:S(2)}) copy-start(bf16[2088,192]{0,1:T(8,128)(2,1)} %reshape.239) | copy-start | bytes 2405380
  883.9 70.9 %copy-start.9 = (bf16[2088,192]{0,1:T(8,128)(2,1)S(1)}, bf16[2088,192]{0,1:T(8,128)(2,1)}, u32[]{:S(2)}) copy-start(bf16[2088,192]{0,1:T(8,128)(2,1)} %reduce-scatter.9.cloned.1.call-done) | copy-start | bytes 2405380
  883.9 70.9 %copy-start.11 = (f32[2088,192]{0,1:T(8,128)S(1)}, f32[2088,192]{0,1:T(8,128)}, u32[]{:S(2)}) copy-start(f32[2088,192]{0,1:T(8,128)} %get-tuple-element.213) | copy-start | bytes 4810756
  883.9 70.9 %copy-start.27 = (f32[2088]{0:T(1024)S(1)}, f32[2088]{0:T(1024)}, u32[]{:S(2)}) copy-start(f32[2088]{0:T(1024)} %copy-done.26) | copy-start | bytes 25060
  883.9 70.9 %copy-start.29 = (f32[2088]{0:T(1024)S(1)}, f32[2088]{0:T(1024)}, u32[]{:S(2)}) copy-start(f32[2088]{0:T(1024)} %copy-done.28) | copy-start | bytes 25060
  883.9 70.9 %copy-start.37 = (f32[2088]{0:T(1024)S(1)}, f32[2088]{0:T(1024)}, u32[]{:S(2)}) copy-start(f32[2088]{0:T(1024)} %copy-done.36) | copy-start | bytes 25060
  884.0 70.9 %copy-start.39 = (f32[2088]{0:T(1024)S(1)}, f32[2088]{0:T(1024)}, u32[]{:S(2)}) copy-start(f32[2088]{0:T(1024)} %copy-done.38) | copy-start | bytes 25060
  884.0 70.9 %copy-start.41 = (f32[192]{0:T(256)S(1)}, f32[192]{0:T(256)}, u32[]{:S(2)}) copy-start(f32[192]{0:T(256)} %param.29) | copy-start | bytes 2308
  884.0 70.9 %copy-start.44 = (f32[192]{0:T(256)S(1)}, f32[192]{0:T(256)}, u32[]{:S(2)}) copy-start(f32[192]{0:T(256)} %param.30) | copy-start | bytes 2308
  (19 other events, 33.1 us)
Sparse Core Ops, SparseCore 0:
  10.3 42.2 all-gather.23
  54.2 28.3 all-gather.13
  85.4 53.1 all-gather.15
  222.3 37.6 reduce-scatter.8
  262.0 53.5 all-gather.25
  317.6 51.7 all-gather.27
  371.6 27.9 all-gather.17
  427.4 39.0 reduce-scatter.10
  513.8 30.2 all-gather.19
  562.4 39.1 reduce-scatter.12
  620.2 30.1 all-gather.21
  761.3 29.3 reduce-scatter.16
  793.0 27.9 reduce-scatter.22
  823.7 27.9 reduce-scatter.20
  853.7 19.3 reduce-scatter.18
  876.1 37.1 all-reduce.8
  915.7 39.0 reduce-scatter.14
